TPU v7x, 32 devices: a whole 2x2x4 slice. The times are simulated.
32 devices in a mesh: wide: 16 (over z, x, core), narrow: 2 (over y).
Axes of the slice: x: 2, y: 2, z: 4, core: 2. Of those that a mesh axis runs over, the one named last changes fastest.
Arguments:
- embeddings: float32 [16384, 512], P(('wide', 'narrow')), may hold values from -2.1 to 2.1
- accum: float32 [16384], P(('wide', 'narrow')), may hold values from 0.01 to 1
- relation: bfloat16 [512, 512], replicated, may hold values from -0.25 to 0.25
- head_index: int32 [2, 16384], P(None, ('wide', 'narrow')), may hold values from 0 to 511
- tail_index: int32 [2, 16384], P(None, ('wide', 'narrow')), may hold values from 0 to 511
- negative_index: int32 [2, 8192], P(None, ('wide', 'narrow')), may hold values from 0 to 511
- partner: int32 [2, 16], replicated, may hold values from 0 to 15, each once within a row
- edge_count: int32 [2, 32], P(None, ('wide', 'narrow')), may hold values from 1 to 512, 8192 in all within a row
Outputs:
- new_embeddings: float32 [16384, 512], P(('wide', 'narrow'))
- new_accum: float32 [16384], P(('wide', 'narrow'))
- relation_grad: float32 [512, 512], replicated
- edge_losses: float32 [2, 16384], P(None, ('wide', 'narrow'))
Inputs may be any that keep to these rules, and one draw needn't show every extreme that they name: Each row of partner is a permutation of the wide indices. `edge_count`: in each bucket step the counts of all devices sum to half of all slots, and some device has exactly 512.
All inputs are finite; a program needn't handle non-finite values.
Results may differ from a plain program's by a relative error of at most 0.0064.
Values may be sent and summed in bfloat16 or wider, within the bound.
A program may use at most 64 MiB of HBM per device.

v0:
```python
import jax
import jax.numpy as jnp
from jax import lax
from jax.sharding import PartitionSpec as P

LEARN_RATE = 0.1
EPSILON = 1e-06


def as_sent(array):

    def short(part):
        return part.astype(jnp.bfloat16) if part.dtype == jnp.float32 else part

    return jax.tree.map(short, array)


def split_rows(values, parts):
    return values.reshape((parts, values.shape[0] // parts) + values.shape[1:])


def join_rows(values):
    return values.reshape((values.shape[0] * values.shape[1],) + values.shape[2:])


def invert(order):
    positions = jnp.arange(order.shape[0], dtype=jnp.int32)
    return jnp.sum(jnp.where(order[:, None] == positions[None, :], positions[:, None], 0), axis=0)


def bucket_terms(query_bf, tail_ids, block_bf, neg_ids):
    tail_rows = jnp.take(block_bf, tail_ids, axis=0)
    own_negs = jnp.take(block_bf, neg_ids, axis=0)
    negatives = lax.all_gather(own_negs, "narrow", axis=0, tiled=True)
    positive = jnp.sum(query_bf.astype(jnp.float32) * tail_rows.astype(jnp.float32), axis=1)
    scores = lax.dot_general(
        query_bf, negatives, (((1,), (1,)), ((), ())), preferred_element_type=jnp.float32
    )
    exp_pos = jnp.exp(positive)
    exp_neg = jnp.exp(scores)
    total = exp_pos + jnp.sum(exp_neg, axis=1)
    losses = jnp.log(total) - positive
    pos_weight = exp_pos / total - 1.0
    weights = (exp_neg / total[:, None]).astype(jnp.bfloat16)
    query_grad = pos_weight[:, None] * tail_rows.astype(jnp.float32) + jnp.dot(
        weights, negatives, preferred_element_type=jnp.float32
    )
    tail_pos = pos_weight[:, None] * query_bf.astype(jnp.float32)
    negative_grad = lax.psum_scatter(
        lax.dot_general(
            weights, query_bf, (((0,), (0,)), ((), ())), preferred_element_type=jnp.float32
        ).astype(jnp.bfloat16),
        "narrow",
        scatter_dimension=0,
        tiled=True,
    ).astype(jnp.float32)
    tail_grad = (
        jnp.zeros(block_bf.shape, jnp.float32)
        .at[tail_ids]
        .add(tail_pos)
        .at[neg_ids]
        .add(negative_grad)
    )
    return (losses, query_grad, tail_grad)


def on_device(
    embeddings, accum, relation, head_index, tail_index, negative_index, partner, edge_count
):
    wide_size = lax.axis_size("wide")
    step_total = head_index.shape[0]
    positions = jnp.arange(head_index.shape[1], dtype=jnp.int32)
    relation_sum = jnp.zeros(relation.shape, jnp.float32)
    loss_rows = []
    for step in range(step_total):
        order = partner[step]
        inverse = invert(order)
        live = positions < edge_count[step, 0]
        block_bf = embeddings.astype(jnp.bfloat16)
        head_rows = jnp.take(block_bf, head_index[step], axis=0)
        query = jnp.dot(head_rows, relation, preferred_element_type=jnp.float32)
        query_bf = jnp.where(live[:, None], query, 0.0).astype(jnp.bfloat16)
        outgoing = lax.all_to_all(
            split_rows(block_bf, wide_size), "wide", split_axis=0, concat_axis=0, tiled=True
        )
        incoming = lax.all_to_all(
            jnp.take(outgoing, order, axis=0), "wide", split_axis=0, concat_axis=0, tiled=True
        )
        losses, query_grad, tail_grad = bucket_terms(
            query_bf, tail_index[step], join_rows(incoming), negative_index[step]
        )
        sent = lax.all_to_all(
            split_rows(tail_grad, wide_size).astype(jnp.bfloat16),
            "wide",
            split_axis=0,
            concat_axis=0,
            tiled=True,
        ).astype(jnp.float32)
        back = lax.all_to_all(
            as_sent(jnp.take(sent, inverse, axis=0)),
            "wide",
            split_axis=0,
            concat_axis=0,
            tiled=True,
        )
        owner_grad = join_rows(back)
        grad_bf = jnp.where(live[:, None], query_grad, 0.0).astype(jnp.bfloat16)
        head_term = lax.dot_general(
            grad_bf, relation, (((1,), (1,)), ((), ())), preferred_element_type=jnp.float32
        )
        head_grad = jnp.zeros(embeddings.shape, jnp.float32).at[head_index[step]].add(head_term)
        relation_part = lax.dot_general(
            head_rows, grad_bf, (((0,), (0,)), ((), ())), preferred_element_type=jnp.float32
        )
        relation_sum = relation_sum + relation_part
        grads = head_grad + owner_grad
        accum = accum + jnp.mean(grads * grads, axis=1)
        embeddings = embeddings - LEARN_RATE * grads / (jnp.sqrt(accum)[:, None] + EPSILON)
        loss_rows.append(jnp.where(live, losses, 0.0))
    relation_sum = lax.psum(relation_sum, ("wide", "narrow"))
    return (embeddings, accum, relation_sum, jnp.stack(loss_rows))


def solution(mesh):
    in_specs = (
        P(("wide", "narrow"), None),
        P(("wide", "narrow")),
        P(),
        P(None, ("wide", "narrow")),
        P(None, ("wide", "narrow")),
        P(None, ("wide", "narrow")),
        P(),
        P(None, ("wide", "narrow")),
    )
    out_specs = (
        P(("wide", "narrow"), None),
        P(("wide", "narrow")),
        P(),
        P(None, ("wide", "narrow")),
    )
    return jax.shard_map(
        on_device, mesh=mesh, in_specs=in_specs, out_specs=out_specs, check_vma=False
    )
```

profile of v0, /device:TPU:0, one launch (start us, length us, event | category | flops | bytes accessed | tf_op | source)
XLA Modules:
  0.0 378.0 jit_solution(17429168418496107216)
XLA Ops:
  7.2 2.1 convert_element_type.88
  9.3 7.5 %all-to-all-start = ((bf16[16,32,512]{2,1,0:T(8,128)(2,1)}), bf16[16,32,512]{2,1,0:T(8,128)(2,1)S(1)}, u32[]{:S(2)}, u32[]{:S(2)}) async-start(bf16[16,32,512]{2,1,0:T(8,128)(2,1)} %bitcast.6), calls=%async_computation | async-start | bytes 1048576 | tf_op jit(solution)/shard_map/all_to_all | solution.py:83
  16.9 3.1 gather_fusion
  21.4 9.7 %all-to-all-done = bf16[16,32,512]{2,1,0:T(8,128)(2,1)S(1)} async-done(((bf16[16,32,512]{2,1,0:T(8,128)(2,1)}), bf16[16,32,512]{2,1,0:T(8,128)(2,1)S(1)}, u32[]{:S(2)}, u32[]{:S(2)}) %all-to-all-start) | async-done | bytes 524320 | tf_op jit(solution)/shard_map/all_to_all | solution.py:83
  32.6 4.2 %all-to-all-start.1 = ((bf16[16,32,512]{2,1,0:T(8,128)(2,1)}), bf16[16,32,512]{2,1,0:T(8,128)(2,1)S(1)}, u32[]{:S(2)}, u32[]{:S(2)}) async-start(bf16[16,32,512]{2,1,0:T(8,128)(2,1)} %broadcast_select_fusion.2), calls=%async_computation.1 | async-start | bytes 1048576 | tf_op jit(solution)/shard_map/all_to_all | solution.py:86
  38.8 12.3 %all-to-all-done.1 = bf16[16,32,512]{2,1,0:T(8,128)(2,1)S(1)} async-done(((bf16[16,32,512]{2,1,0:T(8,128)(2,1)}), bf16[16,32,512]{2,1,0:T(8,128)(2,1)S(1)}, u32[]{:S(2)}, u32[]{:S(2)}) %all-to-all-start.1) | async-done | bytes 524320 | tf_op jit(solution)/shard_map/all_to_all | solution.py:86
  54.5 9.0 %all_gather.6 = bf16[512,512]{1,0:T(8,128)(2,1)S(1)} all-gather(bf16[256,512]{1,0:T(8,128)(2,1)S(1)} %broadcast_select_fusion.7), channel_id=1, replica_groups=mesh['wide'=16,'narrow'=2] {'narrow'}, dimensions={0}, use_global_device_ids=true | all-gather | bytes 786432 | tf_op jit(solution)/shard_map/all_gather | solution.py:34
  68.4 4.5 %scatter_custom_fusion = f32[512,512]{1,0:T(8,128)S(1)} fusion(s32[512]{0:T(512)S(1)} %bitcast.92, f32[512,512]{1,0:T(8,128)} %copy.30, f32[]{:T(128)} %constant.39.clone.1), kind=kCustom, calls=%fused_computation.49 | custom fusion | flops 262144 | bytes 1049088 | tf_op jit(solution)/shard_map/scatter-add | solution.py:60
  72.9 8.6 %reduce-scatter.3.cloned.1.call-done = bf16[256,512]{1,0:T(8,128)(2,1)} async-done(((bf16[512,512]{1,0:T(8,128)(2,1)}), bf16[256,512]{1,0:T(8,128)(2,1)}) %reduce-scatter.3.cloned.1.call-update) | async-done | bytes 262160 | tf_op jit(solution)/shard_map/reduce_scatter | solution.py:49
  81.5 2.9 scatter_custom_fusion.1
  85.2 5.6 %all-to-all-start.2 = ((bf16[16,32,512]{2,1,0:T(8,128)(2,1)}), bf16[16,32,512]{2,1,0:T(8,128)(2,1)S(1)}, u32[]{:S(2)}, u32[]{:S(2)}) async-start(bf16[16,32,512]{2,1,0:T(8,128)(2,1)} %bitcast.11), calls=%async_computation.3 | async-start | bytes 1048576 | tf_op jit(solution)/shard_map/all_to_all | solution.py:92
  91.0 14.1 %all-to-all-done.2 = bf16[16,32,512]{2,1,0:T(8,128)(2,1)S(1)} async-done(((bf16[16,32,512]{2,1,0:T(8,128)(2,1)}), bf16[16,32,512]{2,1,0:T(8,128)(2,1)S(1)}, u32[]{:S(2)}, u32[]{:S(2)}) %all-to-all-start.2) | async-done | bytes 524320 | tf_op jit(solution)/shard_map/all_to_all | solution.py:92
  106.7 4.4 %all-to-all-start.3 = ((bf16[16,32,512]{2,1,0:T(8,128)(2,1)}), bf16[16,32,512]{2,1,0:T(8,128)(2,1)}, u32[]{:S(2)}, u32[]{:S(2)}) async-start(bf16[16,32,512]{2,1,0:T(8,128)(2,1)} %select_convert_fusion.1), calls=%async_computation.4 | async-start | bytes 1048576 | tf_op jit(solution)/shard_map/all_to_all | solution.py:99
  113.4 11.9 %all-to-all-done.3 = bf16[16,32,512]{2,1,0:T(8,128)(2,1)} async-done(((bf16[16,32,512]{2,1,0:T(8,128)(2,1)}), bf16[16,32,512]{2,1,0:T(8,128)(2,1)}, u32[]{:S(2)}, u32[]{:S(2)}) %all-to-all-start.3) | async-done | bytes 524320 | tf_op jit(solution)/shard_map/all_to_all | solution.py:99
  126.5 4.2 %scatter_fusion = f32[512,512]{1,0:T(8,128)S(1)} fusion(f32[512,512]{1,0:T(8,128)S(1)} %bitcast_convert_fusion.1, s32[512]{0:T(512)S(1)} %bitcast.84, f32[512,512]{1,0:T(8,128)S(1)} %fusion.28), kind=kCustom, calls=%fused_computation.12 | custom fusion | flops 262144 | bytes 3147776 | tf_op jit(solution)/shard_map/scatter-add | solution.py:111
  133.0 4.2 %all-to-all-start.4 = ((bf16[16,32,512]{2,1,0:T(8,128)(2,1)}), bf16[16,32,512]{2,1,0:T(8,128)(2,1)S(1)}, u32[]{:S(2)}, u32[]{:S(2)}) async-start(bf16[16,32,512]{2,1,0:T(8,128)(2,1)} %bitcast.21), calls=%async_computation.5 | async-start | bytes 1048576 | tf_op jit(solution)/shard_map/all_to_all | solution.py:83
  137.2 14.2 %all-to-all-done.4 = bf16[16,32,512]{2,1,0:T(8,128)(2,1)S(1)} async-done(((bf16[16,32,512]{2,1,0:T(8,128)(2,1)}), bf16[16,32,512]{2,1,0:T(8,128)(2,1)S(1)}, u32[]{:S(2)}, u32[]{:S(2)}) %all-to-all-start.4) | async-done | bytes 524320 | tf_op jit(solution)/shard_map/all_to_all | solution.py:83
  152.9 4.2 %all-to-all-start.5 = ((bf16[16,32,512]{2,1,0:T(8,128)(2,1)}), bf16[16,32,512]{2,1,0:T(8,128)(2,1)S(1)}, u32[]{:S(2)}, u32[]{:S(2)}) async-start(bf16[16,32,512]{2,1,0:T(8,128)(2,1)} %broadcast_select_fusion), calls=%async_computation.6 | async-start | bytes 1048576 | tf_op jit(solution)/shard_map/all_to_all | solution.py:86
  157.9 3.8 gather_fusion.5
  161.6 9.7 %all-to-all-done.5 = bf16[16,32,512]{2,1,0:T(8,128)(2,1)S(1)} async-done(((bf16[16,32,512]{2,1,0:T(8,128)(2,1)}), bf16[16,32,512]{2,1,0:T(8,128)(2,1)S(1)}, u32[]{:S(2)}, u32[]{:S(2)}) %all-to-all-start.5) | async-done | bytes 524320 | tf_op jit(solution)/shard_map/all_to_all | solution.py:86
  172.5 2.0 gather_fusion.7
  174.9 9.2 %all_gather.7 = bf16[512,512]{1,0:T(8,128)(2,1)S(1)} all-gather(bf16[256,512]{1,0:T(8,128)(2,1)S(1)} %broadcast_select_fusion.6), channel_id=1, replica_groups=mesh['wide'=16,'narrow'=2] {'narrow'}, dimensions={0}, use_global_device_ids=true | all-gather | bytes 786432 | tf_op jit(solution)/shard_map/all_gather | solution.py:34
  190.2 4.5 %scatter_custom_fusion.3 = f32[512,512]{1,0:T(8,128)S(1)} fusion(s32[512]{0:T(512)S(1)} %bitcast.91, f32[512,512]{1,0:T(8,128)} %copy.34, f32[]{:T(128)} %constant.39.clone.1), kind=kCustom, calls=%fused_computation.47 | custom fusion | flops 262144 | bytes 1049088 | tf_op jit(solution)/shard_map/scatter-add | solution.py:60
  194.7 6.5 %reduce-scatter.5.cloned.1.call-done = bf16[256,512]{1,0:T(8,128)(2,1)} async-done(((bf16[512,512]{1,0:T(8,128)(2,1)}), bf16[256,512]{1,0:T(8,128)(2,1)}) %reduce-scatter.5.cloned.1.call-update) | async-done | bytes 262160 | tf_op jit(solution)/shard_map/reduce_scatter | solution.py:49
  201.2 3.1 scatter_custom_fusion.4
  205.2 5.7 %all-to-all-start.6 = ((bf16[16,32,512]{2,1,0:T(8,128)(2,1)}), bf16[16,32,512]{2,1,0:T(8,128)(2,1)}, u32[]{:S(2)}, u32[]{:S(2)}) async-start(bf16[16,32,512]{2,1,0:T(8,128)(2,1)} %bitcast.72), calls=%async_computation.8 | async-start | bytes 1048576 | tf_op jit(solution)/shard_map/all_to_all | solution.py:92
  213.3 11.9 %all-to-all-done.6 = bf16[16,32,512]{2,1,0:T(8,128)(2,1)} async-done(((bf16[16,32,512]{2,1,0:T(8,128)(2,1)}), bf16[16,32,512]{2,1,0:T(8,128)(2,1)}, u32[]{:S(2)}, u32[]{:S(2)}) %all-to-all-start.6) | async-done | bytes 524320 | tf_op jit(solution)/shard_map/all_to_all | solution.py:92
  227.8 4.4 %all-to-all-start.7 = ((bf16[16,32,512]{2,1,0:T(8,128)(2,1)}), bf16[16,32,512]{2,1,0:T(8,128)(2,1)}, u32[]{:S(2)}, u32[]{:S(2)}) async-start(bf16[16,32,512]{2,1,0:T(8,128)(2,1)} %select_convert_fusion), calls=%async_computation.9 | async-start | bytes 1048576 | tf_op jit(solution)/shard_map/all_to_all | solution.py:99
  239.4 7.1 %all-to-all-done.7 = bf16[16,32,512]{2,1,0:T(8,128)(2,1)} async-done(((bf16[16,32,512]{2,1,0:T(8,128)(2,1)}), bf16[16,32,512]{2,1,0:T(8,128)(2,1)}, u32[]{:S(2)}, u32[]{:S(2)}) %all-to-all-start.7) | async-done | bytes 524320 | tf_op jit(solution)/shard_map/all_to_all | solution.py:99
  247.7 4.7 %scatter_fusion.1 = f32[512,512]{1,0:T(8,128)S(1)} fusion(f32[512,512]{1,0:T(8,128)S(1)} %bitcast_convert_fusion, s32[512]{0:T(512)S(1)} %bitcast.83, f32[512,512]{1,0:T(8,128)} %fusion.29), kind=kCustom, calls=%fused_computation.15 | custom fusion | flops 262144 | bytes 3147776 | tf_op jit(solution)/shard_map/scatter-add | solution.py:111
  255.0 114.2 %all-reduce.2.cloned.1.call-done = f32[512,512]{1,0:T(8,128)} async-done(((f32[512,512]{1,0:T(8,128)}), f32[512,512]{1,0:T(8,128)}) %all-reduce.2.cloned.1.call-update) | async-done | bytes 1048592 | tf_op jit(solution)/shard_map/psum | solution.py:120
  369.2 2.3 copy.49
  (133 shorter events, 47.9 us)
Async XLA Ops:
  7.2 56.4 %copy-start = (bf16[512,512]{1,0:T(8,128)(2,1)S(1)}, bf16[512,512]{1,0:T(8,128)(2,1)}, u32[]{:S(2)}) copy-start(bf16[512,512]{1,0:T(8,128)(2,1)} %param.18) | copy-start | bytes 1572868
  9.3 7.5 %copy-start.20 = (s32[2,16]{1,0:T(2,128)S(1)}, s32[2,16]{1,0:T(2,128)}, u32[]{:S(2)}) copy-start(s32[2,16]{1,0:T(2,128)} %param.22) | copy-start | bytes 388
  9.3 7.6 %copy-start.17 = (s32[2,512]{1,0:T(2,128)S(1)}, s32[2,512]{1,0:T(2,128)}, u32[]{:S(2)}) copy-start(s32[2,512]{1,0:T(2,128)} %param.19) | copy-start | bytes 12292
  9.3 21.8 %all-to-all-start = ((bf16[16,32,512]{2,1,0:T(8,128)(2,1)}), bf16[16,32,512]{2,1,0:T(8,128)(2,1)S(1)}, u32[]{:S(2)}, u32[]{:S(2)}) async-start(bf16[16,32,512]{2,1,0:T(8,128)(2,1)} %bitcast.6), calls=%async_computation | async-start | bytes 1048576 | tf_op jit(solution)/shard_map/all_to_all | solution.py:83
  20.0 0.7 copy-start.19
  20.7 0.7 copy-start.16
  32.6 18.4 %all-to-all-start.1 = ((bf16[16,32,512]{2,1,0:T(8,128)(2,1)}), bf16[16,32,512]{2,1,0:T(8,128)(2,1)S(1)}, u32[]{:S(2)}, u32[]{:S(2)}) async-start(bf16[16,32,512]{2,1,0:T(8,128)(2,1)} %broadcast_select_fusion.2), calls=%async_computation.1 | async-start | bytes 1048576 | tf_op jit(solution)/shard_map/all_to_all | solution.py:86
  36.8 44.7 %reduce-scatter.3.cloned.1.call-start = ((), (), s32[]{:S(2)}) async-start(), calls=%async_computation.10 | async-start | bytes 786432 | tf_op jit(solution)/shard_map/reduce_scatter | solution.py:49
  54.4 9.1 %copy-start.15 = (bf16[512,512]{0,1:T(8,128)(2,1)}, bf16[512,512]{0,1:T(8,128)(2,1)S(1)}, u32[]{:S(2)}) copy-start(bf16[512,512]{0,1:T(8,128)(2,1)S(1)} %copy.28) | copy-start | bytes 1572868
  64.6 1.0 copy-start.12
  85.2 19.9 %all-to-all-start.2 = ((bf16[16,32,512]{2,1,0:T(8,128)(2,1)}), bf16[16,32,512]{2,1,0:T(8,128)(2,1)S(1)}, u32[]{:S(2)}, u32[]{:S(2)}) async-start(bf16[16,32,512]{2,1,0:T(8,128)(2,1)} %bitcast.11), calls=%async_computation.3 | async-start | bytes 1048576 | tf_op jit(solution)/shard_map/all_to_all | solution.py:92
  106.7 4.4 %copy-start.13 = (f32[512,512]{0,1:T(8,128)S(1)}, f32[512,512]{0,1:T(8,128)}, u32[]{:S(2)}) copy-start(f32[512,512]{0,1:T(8,128)} %copy-done.12) | copy-start | bytes 3145732
  106.7 18.7 %all-to-all-start.3 = ((bf16[16,32,512]{2,1,0:T(8,128)(2,1)}), bf16[16,32,512]{2,1,0:T(8,128)(2,1)}, u32[]{:S(2)}, u32[]{:S(2)}) async-start(bf16[16,32,512]{2,1,0:T(8,128)(2,1)} %select_convert_fusion.1), calls=%async_computation.4 | async-start | bytes 1048576 | tf_op jit(solution)/shard_map/all_to_all | solution.py:99
  112.6 0.8 copy-start.6
  130.7 0.7 copy-start.18
  130.7 1.2 copy-start.1
  133.0 18.4 %all-to-all-start.4 = ((bf16[16,32,512]{2,1,0:T(8,128)(2,1)}), bf16[16,32,512]{2,1,0:T(8,128)(2,1)S(1)}, u32[]{:S(2)}, u32[]{:S(2)}) async-start(bf16[16,32,512]{2,1,0:T(8,128)(2,1)} %bitcast.21), calls=%async_computation.5 | async-start | bytes 1048576 | tf_op jit(solution)/shard_map/all_to_all | solution.py:83
  152.9 18.4 %all-to-all-start.5 = ((bf16[16,32,512]{2,1,0:T(8,128)(2,1)}), bf16[16,32,512]{2,1,0:T(8,128)(2,1)S(1)}, u32[]{:S(2)}, u32[]{:S(2)}) async-start(bf16[16,32,512]{2,1,0:T(8,128)(2,1)} %broadcast_select_fusion), calls=%async_computation.6 | async-start | bytes 1048576 | tf_op jit(solution)/shard_map/all_to_all | solution.py:86
  157.1 44.1 %reduce-scatter.5.cloned.1.call-start = ((), (), s32[]{:S(2)}) async-start(), calls=%async_computation.11 | async-start | bytes 786432 | tf_op jit(solution)/shard_map/reduce_scatter | solution.py:49
  174.7 9.3 %copy-start.14 = (bf16[512,512]{0,1:T(8,128)(2,1)}, bf16[512,512]{0,1:T(8,128)(2,1)S(1)}, u32[]{:S(2)}) copy-start(bf16[512,512]{0,1:T(8,128)(2,1)S(1)} %copy.32) | copy-start | bytes 1572868
  174.8 9.2 %copy-start.7 = (bf16[512,512]{1,0:T(8,128)(2,1)S(1)}, bf16[512,512]{1,0:T(8,128)(2,1)}, u32[]{:S(2)}) copy-start(bf16[512,512]{1,0:T(8,128)(2,1)} %gather_fusion.5) | copy-start | bytes 1572868
  184.0 0.8 copy-start.3
  184.6 0.8 copy-start.5
  185.3 1.0 copy-start.11
  205.2 20.0 %all-to-all-start.6 = ((bf16[16,32,512]{2,1,0:T(8,128)(2,1)}), bf16[16,32,512]{2,1,0:T(8,128)(2,1)}, u32[]{:S(2)}, u32[]{:S(2)}) async-start(bf16[16,32,512]{2,1,0:T(8,128)(2,1)} %bitcast.72), calls=%async_computation.8 | async-start | bytes 1048576 | tf_op jit(solution)/shard_map/all_to_all | solution.py:92
  227.8 4.4 %copy-start.4 = (bf16[512,512]{1,0:T(8,128)(2,1)S(1)}, bf16[512,512]{1,0:T(8,128)(2,1)}, u32[]{:S(2)}) copy-start(bf16[512,512]{1,0:T(8,128)(2,1)} %copy-done.3) | copy-start | bytes 1572868
  227.8 18.8 %all-to-all-start.7 = ((bf16[16,32,512]{2,1,0:T(8,128)(2,1)}), bf16[16,32,512]{2,1,0:T(8,128)(2,1)}, u32[]{:S(2)}, u32[]{:S(2)}) async-start(bf16[16,32,512]{2,1,0:T(8,128)(2,1)} %select_convert_fusion), calls=%async_computation.9 | async-start | bytes 1048576 | tf_op jit(solution)/shard_map/all_to_all | solution.py:99
  232.2 137.1 %all-reduce.2.cloned.1.call-start = ((), (), s32[]{:S(2)}) async-start(), calls=%async_computation.12 | async-start | bytes 2097152 | tf_op jit(solution)/shard_map/psum | solution.py:120
  232.2 2.7 copy-start.8
  234.2 0.8 copy-start.9
  236.6 1.4 copy-start.10
  252.4 1.2 copy-start.2
  (1 other events, 0.7 us)
Sparse Core Ops, SparseCore 0:
  67.0 14.3 reduce-scatter.2
  187.7 13.4 reduce-scatter.4
  238.2 131.0 all-reduce.1
where the time goes:
time: 380 us; the launch traced here: 378 us
  waiting for transfers between devices  220 us (58%)
  other arithmetic  42.3 us (11%)
  starting transfers between devices  40.2 us (11%)
  local copies, waits for them, and re-layouts  29.1 us (8%)
  blocking collectives  18.2 us (5%)
  between operations  14.4 us (4%)
  matrix products  13.4 us (4%)
    psum x1, waiting for transfers between devices, on_device(): relation_sum = lax.psum(relation_sum, ('wide', 'narrow'))  114 us
    all_to_all x2, waiting for transfers between devices, on_device(): lax.all_to_all(split_rows(tail_grad, wide_size).astype(jnp.bfloat16), 'wi...  26.1 us
    all_to_all x2, waiting for transfers between devices, on_device(): lax.all_to_all(split_rows(block_bf, wide_size), 'wide', split_axis=0, con...  23.9 us
    all_to_all x2, waiting for transfers between devices, on_device(): lax.all_to_all(jnp.take(outgoing, order, axis=0), 'wide', split_axis=0, c...  22 us
    all_to_all x2, waiting for transfers between devices, on_device(): lax.all_to_all(as_sent(jnp.take(sent, inverse, axis=0)), 'wide', split_ax...  19.1 us
    all_gather x2, blocking collectives, bucket_terms(): negatives = lax.all_gather(own_negs, 'narrow', axis=0, tiled=True)  18.2 us
    scatter-add x4, other arithmetic, bucket_terms(): tail_grad = jnp.zeros(block_bf.shape, jnp.float32).at[tail_ids].add(tail_...  15.1 us
    reduce_scatter x2, waiting for transfers between devices, bucket_terms(): lax.psum_scatter(lax.dot_general(weights, query_bf, (((0,), (0,)), ((), (...  15.1 us
  transfers between devices with their start and end apart: 11, of which 11 were waited for; matrix products, arithmetic and copies ran while one was open for 11% of the time, Pallas kernels for 0%

commit v1 on v0

v1 whole, which is shorter than its diff:
```python
import functools

import jax
import jax.numpy as jnp
from jax import lax
from jax.experimental import pallas as pl
from jax.experimental.pallas import tpu as pltpu
from jax.sharding import PartitionSpec as P

LEARN_RATE = 0.1
EPSILON = 1e-06
MESH = pl.DeviceIdType.MESH
F32 = jnp.float32
BF16 = jnp.bfloat16

QUERY_OUT, QUERY_IN, GRAD_OUT, GRAD_IN, LOSS = range(5)
NEG, NEG_GRAD = range(2)
TAIL_IDS, NEG_IDS, REL_SUM, REL_GROUP, REL_ALL = range(5)


def dot(a, b, contract):
    return lax.dot_general(a, b, (contract, ((), ())), preferred_element_type=F32)


def one_hot_t(row, rows):
    number = lax.broadcasted_iota(jnp.int32, (rows, row.shape[1]), 0)
    return jnp.where(number == row, 1.0, 0.0).astype(BF16)


def to_row(column):
    return jnp.transpose(jnp.broadcast_to(column, (column.shape[0], 128)))[:1, :]


def to_column(row):
    return jnp.transpose(jnp.broadcast_to(row, (128, row.shape[1])))[:, :1]


def kernel(
    wide, narrow, chunk,
    emb_ref, acc_ref, rel_ref, head_ref, tail_ref, neg_ref, partner_ref, inverse_ref, count_ref,
    emb_out, acc_out, rel_out, loss_out,
    tail_all, neg_all, table, head_t, tail_t, neg_t, head_rows, tail_rows,
    q_send, q_mid, q_mid_send, q_recv, g_send, g_mid, g_mid_send, g_recv,
    loss_send, loss_all, negs, ng_send, ng_recv, weights, tail_pos, tail_grad,
    rel_acc, rel_send, rel_recv, rel_group_send, rel_group, rel_all_send, rel_all,
    send_sem, recv_sem, nsend_sem, nrecv_sem, xsend_sem, xrecv_sem,
):
    w = lax.axis_index("wide")
    n = lax.axis_index("narrow")
    steps, edges = head_ref.shape
    block, width = emb_ref.shape
    negatives = neg_ref.shape[1]

    barrier = pltpu.get_barrier_semaphore()

    def greet_wide(i, carry):
        pl.semaphore_signal(
            barrier, inc=1, device_id=(lax.rem(w + i, wide), n), device_id_type=MESH
        )
        return carry

    def greet_narrow(i, carry):
        pl.semaphore_signal(
            barrier, inc=1, device_id=(w, lax.rem(n + i, narrow)), device_id_type=MESH
        )
        return carry

    lax.fori_loop(1, wide, greet_wide, 0)
    lax.fori_loop(1, narrow, greet_narrow, 0)
    pl.semaphore_wait(barrier, wide + narrow - 2)

    def wide_start(source, target, ssem, rsem):
        def go(i, carry):
            j = lax.rem(w + i, wide)
            pltpu.make_async_remote_copy(
                src_ref=source(j), dst_ref=target(w), send_sem=ssem, recv_sem=rsem,
                device_id=(j, n), device_id_type=MESH,
            ).start()
            return carry

        lax.fori_loop(1, wide, go, 0)

    def narrow_start(source, target, ssem, rsem):
        def go(i, carry):
            j = lax.rem(n + i, narrow)
            pltpu.make_async_remote_copy(
                src_ref=source(j), dst_ref=target(n), send_sem=ssem, recv_sem=rsem,
                device_id=(w, j), device_id_type=MESH,
            ).start()
            return carry

        lax.fori_loop(1, narrow, go, 0)

    def wait(slots, sem):
        pltpu.make_async_copy(slots, slots, sem).wait()

    wide_start(
        lambda j: tail_ref, lambda m: tail_all.at[m], xsend_sem.at[TAIL_IDS], xrecv_sem.at[TAIL_IDS]
    )
    wide_start(
        lambda j: neg_ref, lambda m: neg_all.at[m], xsend_sem.at[NEG_IDS], xrecv_sem.at[NEG_IDS]
    )
    tail_all[w] = tail_ref[...]
    neg_all[w] = neg_ref[...]
    emb_out[...] = emb_ref[...]
    acc_out[...] = acc_ref[...]
    rel_acc[...] = jnp.zeros_like(rel_acc)
    others = pl.ds(0, wide - 1)
    peers = pl.ds(0, narrow - 1)

    def step(s, carry):
        row = pl.ds(s, 1)
        count = count_ref[s, 0]
        table[...] = emb_out[...].astype(BF16)
        head_t[...] = one_hot_t(head_ref[row, :], block)
        head_rows[...] = dot(head_t[...], table[...], ((0,), (0,))).astype(BF16)
        query = dot(head_rows[...], rel_ref[...], ((1,), (0,)))
        live = lax.broadcasted_iota(jnp.int32, (edges, width), 0) < count
        q_send[s] = jnp.where(live, query, 0.0).astype(BF16).reshape(q_send.shape[1:])
        wide_start(
            lambda j: q_send.at[s, j], lambda m: q_mid.at[s, m],
            send_sem.at[s, QUERY_OUT], recv_sem.at[s, QUERY_OUT],
        )
        q_mid[s, w] = q_send[s, w]

        @pl.when(s == 0)
        def _():
            wait(tail_all.at[others], xrecv_sem.at[TAIL_IDS])
            wait(neg_all.at[others], xrecv_sem.at[NEG_IDS])

        user = inverse_ref[s, w]
        neg_t[...] = one_hot_t(neg_all[user, row, :], block)
        negs[s, n] = dot(neg_t[...], table[...], ((0,), (0,))).astype(BF16)
        narrow_start(
            lambda j: negs.at[s, n], lambda m: negs.at[s, m],
            nsend_sem.at[s, NEG], nrecv_sem.at[s, NEG],
        )
        tail_t[...] = one_hot_t(tail_all[user, row, :], block)
        tail_rows[...] = dot(tail_t[...], table[...], ((0,), (0,))).astype(BF16)

        wait(q_mid.at[s, others], recv_sem.at[s, QUERY_OUT])

        def relay_query(j, c):
            q_mid_send[s, j] = q_mid[s, inverse_ref[s, j]]
            return c

        lax.fori_loop(0, wide, relay_query, 0)
        wide_start(
            lambda j: q_mid_send.at[s, j], lambda m: q_recv.at[s, m],
            send_sem.at[s, QUERY_IN], recv_sem.at[s, QUERY_IN],
        )
        q_recv[s, w] = q_mid_send[s, w]
        wait(negs.at[s, peers], nrecv_sem.at[s, NEG])
        wait(q_recv.at[s, others], recv_sem.at[s, QUERY_IN])

        shared = negs[s].reshape(narrow * negatives, width)
        pieces = chunk // q_recv.shape[2]
        for c in range(edges // chunk):
            part = slice(c * chunk, (c + 1) * chunk)
            part3 = slice(c * pieces, (c + 1) * pieces)
            q = q_recv[s, part3].reshape(chunk, width)
            q32 = q.astype(F32)
            t32 = tail_rows[part, :].astype(F32)
            positive = jnp.sum(q32 * t32, axis=1, keepdims=True)
            exp_neg = jnp.exp(dot(q, shared, ((1,), (1,))))
            exp_pos = jnp.exp(positive)
            total = exp_pos + jnp.sum(exp_neg, axis=1, keepdims=True)
            pos_weight = exp_pos / total - 1.0
            wts = (exp_neg * (1.0 / total)).astype(BF16)
            weights[part, :] = wts
            grad = pos_weight * t32 + dot(wts, shared, ((1,), (0,)))
            g_send[s, part3] = grad.astype(BF16).reshape(pieces, q_recv.shape[2], width)
            tail_pos[part, :] = (pos_weight * q32).astype(BF16)
            loss_send[s, :, part] = to_row(jnp.log(total) - positive)
        wide_start(
            lambda j: g_send.at[s, j], lambda m: g_mid.at[s, m],
            send_sem.at[s, GRAD_OUT], recv_sem.at[s, GRAD_OUT],
        )
        g_mid[s, w] = g_send[s, w]
        queries = q_recv[s].reshape(edges, width)
        for k in range(narrow):
            cols = slice(k * negatives, (k + 1) * negatives)
            ng_send[s, k] = dot(weights[:, cols], queries, ((0,), (0,))).astype(BF16)
        narrow_start(
            lambda j: ng_send.at[s, j], lambda m: ng_recv.at[s, m],
            nsend_sem.at[s, NEG_GRAD], nrecv_sem.at[s, NEG_GRAD],
        )
        ng_recv[s, n] = ng_send[s, n]
        wide_start(
            lambda j: loss_send.at[s], lambda m: loss_all.at[s, m],
            send_sem.at[s, LOSS], recv_sem.at[s, LOSS],
        )
        loss_all[s, w] = loss_send[s]
        tail_grad[...] = dot(tail_t[...], tail_pos[...], ((1,), (0,)))

        wait(g_mid.at[s, others], recv_sem.at[s, GRAD_OUT])

        def relay_grad(j, c):
            g_mid_send[s, j] = g_mid[s, partner_ref[s, j]]
            return c

        lax.fori_loop(0, wide, relay_grad, 0)
        wide_start(
            lambda j: g_mid_send.at[s, j], lambda m: g_recv.at[s, m],
            send_sem.at[s, GRAD_IN], recv_sem.at[s, GRAD_IN],
        )
        g_recv[s, w] = g_mid_send[s, w]

        wait(ng_recv.at[s, peers], nrecv_sem.at[s, NEG_GRAD])
        for k in range(narrow):
            tail_grad[...] += dot(neg_t[...], ng_recv[s, k], ((1,), (0,)))
        wait(loss_all.at[s, others], recv_sem.at[s, LOSS])
        losses = loss_all[s, partner_ref[s, w]]
        live_row = lax.broadcasted_iota(jnp.int32, (1, edges), 1) < count
        loss_out[row, :] = jnp.where(live_row, losses, 0.0)

        wait(g_recv.at[s, others], recv_sem.at[s, GRAD_IN])
        back = g_recv[s].reshape(edges, width)
        grad_bf = jnp.where(live, back.astype(F32), 0.0).astype(BF16)
        rel_acc[...] += dot(head_rows[...], grad_bf, ((0,), (0,)))

        @pl.when(s == steps - 1)
        def _():
            rel_send[...] = rel_acc[...].astype(BF16).reshape(rel_send.shape)
            wide_start(
                lambda j: rel_send.at[j], lambda m: rel_recv.at[m],
                xsend_sem.at[REL_SUM], xrecv_sem.at[REL_SUM],
            )
            rel_recv[w] = rel_send[w]

        head_term = dot(grad_bf, rel_ref[...], ((1,), (1,))).astype(BF16)
        grads = tail_grad[...] + dot(head_t[...], head_term, ((1,), (0,)))
        acc = to_column(acc_out[...]) + jnp.mean(grads * grads, axis=1, keepdims=True)
        acc_out[...] = to_row(acc)
        emb_out[...] = emb_out[...] - grads * (LEARN_RATE / (jnp.sqrt(acc) + EPSILON))

        wait(q_send.at[s, others], send_sem.at[s, QUERY_OUT])
        wait(q_send.at[s, others], send_sem.at[s, QUERY_IN])
        wait(q_send.at[s, others], send_sem.at[s, GRAD_OUT])
        wait(q_send.at[s, others], send_sem.at[s, GRAD_IN])
        wait(loss_all.at[s, others], send_sem.at[s, LOSS])
        wait(negs.at[s, peers], nsend_sem.at[s, NEG])
        wait(negs.at[s, peers], nsend_sem.at[s, NEG_GRAD])
        return carry

    lax.fori_loop(0, steps, step, 0)

    wait(rel_recv.at[others], xrecv_sem.at[REL_SUM])
    mine = rel_recv[0].astype(F32)
    for j in range(1, wide):
        mine = mine + rel_recv[j].astype(F32)
    rel_group_send[...] = mine
    narrow_start(
        lambda j: rel_group_send, lambda m: rel_group.at[m],
        xsend_sem.at[REL_GROUP], xrecv_sem.at[REL_GROUP],
    )
    rel_group[n] = mine
    wait(rel_group.at[peers], xrecv_sem.at[REL_GROUP])
    summed = rel_group[0]
    for k in range(1, narrow):
        summed = summed + rel_group[k]
    rel_all_send[...] = summed.astype(BF16)
    wide_start(
        lambda j: rel_all_send, lambda m: rel_all.at[m],
        xsend_sem.at[REL_ALL], xrecv_sem.at[REL_ALL],
    )
    rel_all[w] = rel_all_send[...]
    wait(rel_all.at[others], xrecv_sem.at[REL_ALL])
    rel_out[...] = rel_all[...].astype(F32).reshape(rel_out.shape)

    wait(tail_all.at[others], xsend_sem.at[TAIL_IDS])
    wait(neg_all.at[others], xsend_sem.at[NEG_IDS])
    wait(rel_recv.at[others], xsend_sem.at[REL_SUM])
    wait(rel_group.at[peers], xsend_sem.at[REL_GROUP])
    wait(rel_all.at[others], xsend_sem.at[REL_ALL])


def invert(order):
    positions = jnp.arange(order.shape[1], dtype=jnp.int32)
    return jnp.sum(
        jnp.where(order[:, :, None] == positions, positions[:, None], 0), axis=1, dtype=jnp.int32
    )


def on_device(
    wide, narrow,
    embeddings, accum, relation, head_index, tail_index, negative_index, partner, edge_count
):
    steps, edges = head_index.shape
    block, width = embeddings.shape
    negatives = negative_index.shape[1]
    piece = edges // wide
    depth = width // wide
    chunk = min(edges, 256)
    vmem = pl.BlockSpec(memory_space=pltpu.VMEM)
    smem = pl.BlockSpec(memory_space=pltpu.SMEM)
    pieces = pltpu.VMEM((steps, wide, piece, width), BF16)
    group = pltpu.VMEM((steps, narrow, negatives, width), BF16)
    sems = pltpu.SemaphoreType.DMA
    new_emb, new_acc, rel_grad, losses = pl.pallas_call(
        functools.partial(kernel, wide, narrow, chunk),
        out_shape=(
            jax.ShapeDtypeStruct(embeddings.shape, F32),
            jax.ShapeDtypeStruct((1, block), F32),
            jax.ShapeDtypeStruct(relation.shape, F32),
            jax.ShapeDtypeStruct((steps, edges), F32),
        ),
        in_specs=[vmem] * 6 + [smem] * 3,
        out_specs=(vmem,) * 4,
        scratch_shapes=[
            pltpu.VMEM((wide, steps, edges), jnp.int32),
            pltpu.VMEM((wide, steps, negatives), jnp.int32),
            pltpu.VMEM((block, width), BF16),
            pltpu.VMEM((block, edges), BF16),
            pltpu.VMEM((block, edges), BF16),
            pltpu.VMEM((block, negatives), BF16),
            pltpu.VMEM((edges, width), BF16),
            pltpu.VMEM((edges, width), BF16),
            *([pieces] * 8),
            pltpu.VMEM((steps, 1, edges), F32),
            pltpu.VMEM((steps, wide, 1, edges), F32),
            group, group, group,
            pltpu.VMEM((edges, narrow * negatives), BF16),
            pltpu.VMEM((edges, width), BF16),
            pltpu.VMEM((block, width), F32),
            pltpu.VMEM(relation.shape, F32),
            pltpu.VMEM((wide, depth, width), BF16),
            pltpu.VMEM((wide, depth, width), BF16),
            pltpu.VMEM((depth, width), F32),
            pltpu.VMEM((narrow, depth, width), F32),
            pltpu.VMEM((depth, width), BF16),
            pltpu.VMEM((wide, depth, width), BF16),
            sems((steps, 5)), sems((steps, 5)), sems((steps, 2)), sems((steps, 2)),
            sems((5,)), sems((5,)),
        ],
        compiler_params=pltpu.CompilerParams(
            collective_id=0, has_side_effects=True, vmem_limit_bytes=56 * 1024 * 1024
        ),
    )(
        embeddings, accum.reshape(1, block), relation, head_index, tail_index, negative_index,
        partner, invert(partner), edge_count,
    )
    return new_emb, new_acc.reshape(block), rel_grad, losses


def solution(mesh):
    both = ("wide", "narrow")
    in_specs = (
        P(both, None), P(both), P(), P(None, both), P(None, both), P(None, both), P(), P(None, both)
    )
    out_specs = (P(both, None), P(both), P(), P(None, both))
    return jax.shard_map(
        functools.partial(on_device, mesh.shape["wide"], mesh.shape["narrow"]),
        mesh=mesh, in_specs=in_specs, out_specs=out_specs, check_vma=False,
    )
```

time: 380 us -> 150 us (0.39)
  waiting for transfers between devices: 220 us -> 0 us
  Pallas kernels: 0 us -> 141 us
  other arithmetic: 42.3 us -> 0.65 us
  starting transfers between devices: 40.2 us -> 0 us
  local copies, waits for them, and re-layouts: 29.1 us -> 5.83 us
  blocking collectives: 18.2 us -> 0 us
  between operations: 14.4 us -> 0.67 us
  matrix products: 13.4 us -> 0 us
    pallas_call x0 -> x1, Pallas kernels: none -> 141 us  [on_device(): pl.pallas_call(functools.partial(kernel, wide, narrow, chunk), out_shape=...]
    psum x1 -> x0, waiting for transfers between devices: 114 us -> none  [on_device(): relation_sum = lax.psum(relation_sum, ('wide', 'narrow'))]
    all_to_all x8 -> x0, waiting for transfers between devices: 91.1 us -> none  [the longest x2 26.1 us: on_device(): lax.all_to_all(split_rows(tail_grad, wide_size).astype(jnp.bfloat16), 'wi...]
    all_to_all x8 -> x0, starting transfers between devices: 40.1 us -> none  [the longest x2 11.7 us: on_device(): lax.all_to_all(split_rows(block_bf, wide_size), 'wide', split_axis=0, con...]
    scatter-add x6 -> x0, other arithmetic: 23.9 us -> none  [the longest x4 15.1 us: bucket_terms(): tail_grad = jnp.zeros(block_bf.shape, jnp.float32).at[tail_ids].add(tail_...]
    all_gather x2 -> x0, blocking collectives: 18.2 us -> none  [bucket_terms(): negatives = lax.all_gather(own_negs, 'narrow', axis=0, tiled=True)]
    gather x12 -> x0, local copies, waits for them, and re-layouts: 16.9 us -> none  [the longest x2 6.86 us: on_device(): head_rows = jnp.take(block_bf, head_index[step], axis=0)]
    reduce_scatter x2 -> x0, waiting for transfers between devices: 15.1 us -> none  [bucket_terms(): lax.psum_scatter(lax.dot_general(weights, query_bf, (((0,), (0,)), ((), (...]
  transfers between devices with their start and end apart: 11 -> 0, of which waited for: 11 -> 0; matrix products, arithmetic and copies ran while one was open for 11% -> 0% of each run, Pallas kernels for 0% -> 0%
where the time goes in v1:
time: 150 us; the launch traced here: 149 us
  Pallas kernels  141 us (94%)
  local copies, waits for them, and re-layouts  5.83 us (4%)
    pallas_call x1, Pallas kernels, on_device(): pl.pallas_call(functools.partial(kernel, wide, narrow, chunk), out_shape=...  141 us
    unnamed x15, local copies, waits for them, and re-layouts  5.83 us

profile of v1, /device:TPU:0, one launch (start us, length us, event | category | flops | bytes accessed | tf_op | source)
XLA Modules:
  0.0 148.6 jit_solution(6211721645557368336)
XLA Ops:
  0.6 0.0 copy-start.4
  0.6 0.6 copy-done.4
  1.3 0.0 copy-start.2
  1.3 0.6 copy.13.count_ref
  1.9 0.0 copy-done.2
  2.0 0.6 select_reduce_fusion.inverse_ref
  2.6 141.5 %shard_map.111 = (f32[512,512]{1,0:T(8,128)}, f32[1,512]{1,0:T(1,128)}, f32[512,512]{1,0:T(8,128)}, f32[2,512]{1,0:T(2,128)}) custom-call(f32[512,512]{1,0:T(8,128)} %emb_ref.1, f32[1,512]{1,0:T(1,128)} %bitcast.2, bf16[512,512]{1,0:T(8,128)(2,1)} %rel_ref.1, s32[2,512]{1,0:T(2,128)} %head_ref.1, s32[2,512]{1,0:T(2,128)} %tail_ref.1, s32[2,256]{1,0:T(2,128)} %neg_ref.1, ...), custom_call_target="tpu_custom_call" | custom-call | tf_op jit(solution)/shard_map/pallas_call | solution.py:300
  144.1 0.0 copy-start.3
  144.1 0.0 copy-start
  144.1 2.4 %copy.18 = f32[512,512]{1,0:T(8,128)} copy(f32[512,512]{1,0:T(8,128)} %get-tuple-element.16) | data formatting | bytes 2097152
  146.5 0.0 copy-done.3
  146.5 0.6 copy.19
  147.1 0.0 copy-done
  147.1 0.0 copy-start.1
  147.1 1.0 copy.20
  148.0 0.0 copy-done.1
  148.0 0.6 copy.21
Async XLA Ops:
  0.6 0.7 copy-start.4
  1.3 0.7 copy-start.2
  144.1 2.4 %copy-start.3 = (f32[1,512]{1,0:T(1,128)S(1)}, f32[1,512]{1,0:T(1,128)}, u32[]{:S(2)}) copy-start(f32[1,512]{1,0:T(1,128)} %get-tuple-element.9) | copy-start | bytes 6148
  144.1 2.9 %copy-start = (f32[512,512]{1,0:T(8,128)S(1)}, f32[512,512]{1,0:T(8,128)}, u32[]{:S(2)}) copy-start(f32[512,512]{1,0:T(8,128)} %get-tuple-element.18) | copy-start | bytes 3145732
  147.1 1.0 copy-start.1

commit v2 on v1

v2 whole, which is shorter than its diff:
```python
import functools

import jax
import jax.numpy as jnp
from jax import lax
from jax.experimental import pallas as pl
from jax.experimental.pallas import tpu as pltpu
from jax.sharding import PartitionSpec as P

LEARN_RATE = 0.1
EPSILON = 1e-06
MESH = pl.DeviceIdType.MESH
F32 = jnp.float32
BF16 = jnp.bfloat16

QUERY_OUT, QUERY_IN, GRAD_OUT, GRAD_IN, LOSS = range(5)
NEG, NEG_GRAD = range(2)
TAIL_IDS, NEG_IDS, REL_SUM, REL_GROUP, REL_ALL = range(5)
HALVES = 2


def dot(a, b, contract):
    return lax.dot_general(a, b, (contract, ((), ())), preferred_element_type=F32)


def one_hot_t(row, rows):
    number = lax.broadcasted_iota(jnp.int32, (rows, row.shape[1]), 0)
    return jnp.where(number == row, 1.0, 0.0).astype(BF16)


def to_row(column):
    return jnp.transpose(jnp.broadcast_to(column, (column.shape[0], 128)))[:1, :]


def to_column(row):
    return jnp.transpose(jnp.broadcast_to(row, (128, row.shape[1])))[:, :1]


def kernel(
    wide, narrow, chunk,
    emb_ref, acc_ref, rel_ref, head_ref, tail_ref, neg_ref, partner_ref, inverse_ref, count_ref,
    emb_out, acc_out, rel_out, loss_out,
    tail_all, neg_all, table, head_t, tail_t, neg_t, head_rows, tail_rows,
    q_send, q_mid, q_mid_send, q_recv, g_send, g_mid, g_mid_send, g_recv,
    loss_send, loss_all, negs, ng_send, ng_recv, weights, tail_pos, tail_grad,
    rel_acc, rel_send, rel_recv, rel_group_send, rel_group, rel_all_send, rel_all,
    send_sem, recv_sem, nsend_sem, nrecv_sem, xsend_sem, xrecv_sem,
):
    w = lax.axis_index("wide")
    n = lax.axis_index("narrow")
    steps, edges = head_ref.shape
    block, width = emb_ref.shape
    negatives = neg_ref.shape[1]
    parts = edges // chunk
    half = width // HALVES

    barrier = pltpu.get_barrier_semaphore()

    def greet_wide(i, carry):
        pl.semaphore_signal(
            barrier, inc=1, device_id=(lax.rem(w + i, wide), n), device_id_type=MESH
        )
        return carry

    def greet_narrow(i, carry):
        pl.semaphore_signal(
            barrier, inc=1, device_id=(w, lax.rem(n + i, narrow)), device_id_type=MESH
        )
        return carry

    lax.fori_loop(1, wide, greet_wide, 0)
    lax.fori_loop(1, narrow, greet_narrow, 0)
    pl.semaphore_wait(barrier, wide + narrow - 2)

    def wide_start(source, target, ssem, rsem):
        def go(i, carry):
            j = lax.rem(w + i, wide)
            pltpu.make_async_remote_copy(
                src_ref=source(j), dst_ref=target(w), send_sem=ssem, recv_sem=rsem,
                device_id=(j, n), device_id_type=MESH,
            ).start()
            return carry

        lax.fori_loop(1, wide, go, 0)

    def narrow_start(source, target, ssem, rsem):
        def go(i, carry):
            j = lax.rem(n + i, narrow)
            pltpu.make_async_remote_copy(
                src_ref=source(j), dst_ref=target(n), send_sem=ssem, recv_sem=rsem,
                device_id=(w, j), device_id_type=MESH,
            ).start()
            return carry

        lax.fori_loop(1, narrow, go, 0)

    def wait(slots, sem):
        pltpu.make_async_copy(slots, slots, sem).wait()

    def exchange(source, target, s, c, phase):
        wide_start(
            lambda j: source.at[s, c, j], lambda m: target.at[s, m],
            send_sem.at[s, c, phase], recv_sem.at[s, c, phase],
        )
        target[s, w] = source[s, c, w]

    wide_start(
        lambda j: tail_ref, lambda m: tail_all.at[m], xsend_sem.at[0, TAIL_IDS], xrecv_sem.at[0, TAIL_IDS]
    )
    wide_start(
        lambda j: neg_ref, lambda m: neg_all.at[m], xsend_sem.at[0, NEG_IDS], xrecv_sem.at[0, NEG_IDS]
    )
    tail_all[w] = tail_ref[...]
    neg_all[w] = neg_ref[...]
    emb_out[...] = emb_ref[...]
    acc_out[...] = acc_ref[...]
    rel_acc[...] = jnp.zeros_like(rel_acc)
    others = pl.ds(0, wide - 1)
    peers = pl.ds(0, narrow - 1)

    def step(s, carry):
        row = pl.ds(s, 1)
        count = count_ref[s, 0]
        table[...] = emb_out[...].astype(BF16)
        head_t[...] = one_hot_t(head_ref[row, :], block)
        for c in range(parts):
            part = slice(c * chunk, (c + 1) * chunk)
            rows = dot(head_t[:, part], table[...], ((0,), (0,))).astype(BF16)
            head_rows[part, :] = rows
            query = dot(rows, rel_ref[...], ((1,), (0,)))
            live = lax.broadcasted_iota(jnp.int32, (chunk, width), 0) + c * chunk < count
            q_send[s, c] = jnp.where(live, query, 0.0).astype(BF16).reshape(q_send.shape[2:])
            exchange(q_send, q_mid[c], s, c, QUERY_OUT)
        @pl.when(s == 0)
        def _():
            wait(tail_all.at[others], xrecv_sem.at[0, TAIL_IDS])
            wait(neg_all.at[others], xrecv_sem.at[0, NEG_IDS])

        user = inverse_ref[s, w]
        neg_t[...] = one_hot_t(neg_all[user, row, :], block)
        negs[s, n] = dot(neg_t[...], table[...], ((0,), (0,))).astype(BF16)
        narrow_start(
            lambda j: negs.at[s, n], lambda m: negs.at[s, m],
            nsend_sem.at[s, NEG], nrecv_sem.at[s, NEG],
        )
        tail_t[...] = one_hot_t(tail_all[user, row, :], block)
        tail_rows[...] = dot(tail_t[...], table[...], ((0,), (0,))).astype(BF16)

        for c in range(parts):
            wait(q_mid[c].at[s, others], recv_sem.at[s, c, QUERY_OUT])

            def relay_query(j, carry, c=c):
                q_mid_send[s, c, j] = q_mid[c][s, inverse_ref[s, j]]
                return carry

            lax.fori_loop(0, wide, relay_query, 0)
            exchange(q_mid_send, q_recv[c], s, c, QUERY_IN)
        wait(negs.at[s, peers], nrecv_sem.at[s, NEG])

        shared = negs[s].reshape(narrow * negatives, width)
        for c in range(parts):
            part = slice(c * chunk, (c + 1) * chunk)
            wait(q_recv[c].at[s, others], recv_sem.at[s, c, QUERY_IN])
            q = q_recv[c][s].reshape(chunk, width)
            q32 = q.astype(F32)
            t32 = tail_rows[part, :].astype(F32)
            positive = jnp.sum(q32 * t32, axis=1, keepdims=True)
            exp_neg = jnp.exp(dot(q, shared, ((1,), (1,))))
            exp_pos = jnp.exp(positive)
            total = exp_pos + jnp.sum(exp_neg, axis=1, keepdims=True)
            pos_weight = exp_pos / total - 1.0
            wts = (exp_neg * (1.0 / total)).astype(BF16)
            weights[part, :] = wts
            grad = pos_weight * t32 + dot(wts, shared, ((1,), (0,)))
            g_send[s, c] = grad.astype(BF16).reshape(g_send.shape[2:])
            exchange(g_send, g_mid[c], s, c, GRAD_OUT)
            tail_pos[part, :] = (pos_weight * q32).astype(BF16)
            loss_send[s, :, part] = to_row(jnp.log(total) - positive)
        for k in range(narrow):
            cols = slice(k * negatives, (k + 1) * negatives)
            term = jnp.zeros((negatives, width), F32)
            for c in range(parts):
                part = slice(c * chunk, (c + 1) * chunk)
                queries = q_recv[c][s].reshape(chunk, width)
                term = term + dot(weights[part, cols], queries, ((0,), (0,)))
            ng_send[s, k] = term.astype(BF16)
        narrow_start(
            lambda j: ng_send.at[s, j], lambda m: ng_recv.at[s, m],
            nsend_sem.at[s, NEG_GRAD], nrecv_sem.at[s, NEG_GRAD],
        )
        ng_recv[s, n] = ng_send[s, n]
        wide_start(
            lambda j: loss_send.at[s], lambda m: loss_all.at[s, m],
            send_sem.at[s, 0, LOSS], recv_sem.at[s, 0, LOSS],
        )
        loss_all[s, w] = loss_send[s]
        tail_grad[...] = dot(tail_t[...], tail_pos[...], ((1,), (0,)))

        for c in range(parts):
            wait(g_mid[c].at[s, others], recv_sem.at[s, c, GRAD_OUT])

            def relay_grad(j, carry, c=c):
                g_mid_send[s, c, j] = g_mid[c][s, partner_ref[s, j]]
                return carry

            lax.fori_loop(0, wide, relay_grad, 0)
            exchange(g_mid_send, g_recv[c], s, c, GRAD_IN)

        wait(ng_recv.at[s, peers], nrecv_sem.at[s, NEG_GRAD])
        for k in range(narrow):
            tail_grad[...] += dot(neg_t[...], ng_recv[s, k], ((1,), (0,)))
        wait(loss_all.at[s, others], recv_sem.at[s, 0, LOSS])
        losses = loss_all[s, partner_ref[s, w]]
        live_row = lax.broadcasted_iota(jnp.int32, (1, edges), 1) < count
        loss_out[row, :] = jnp.where(live_row, losses, 0.0)

        for c in range(parts):
            part = slice(c * chunk, (c + 1) * chunk)
            wait(g_recv[c].at[s, others], recv_sem.at[s, c, GRAD_IN])
            back = g_recv[c][s].reshape(chunk, width).astype(F32)
            live = lax.broadcasted_iota(jnp.int32, (chunk, width), 0) + c * chunk < count
            grad_bf = jnp.where(live, back, 0.0).astype(BF16)
            rel_acc[...] += dot(head_rows[part, :], grad_bf, ((0,), (0,)))
            tail_pos[part, :] = dot(grad_bf, rel_ref[...], ((1,), (1,))).astype(BF16)

        @pl.when(s == steps - 1)
        def _():
            for h in range(HALVES):
                cols = slice(h * half, (h + 1) * half)
                rel_send[h] = rel_acc[:, cols].astype(BF16).reshape(rel_send.shape[1:])
                wide_start(
                    lambda j: rel_send.at[h, j], lambda m: rel_recv.at[h, m],
                    xsend_sem.at[h, REL_SUM], xrecv_sem.at[h, REL_SUM],
                )
                rel_recv[h, w] = rel_send[h, w]

        grads = tail_grad[...] + dot(head_t[...], tail_pos[...], ((1,), (0,)))
        acc = to_column(acc_out[...]) + jnp.mean(grads * grads, axis=1, keepdims=True)
        acc_out[...] = to_row(acc)
        emb_out[...] = emb_out[...] - grads * (LEARN_RATE / (jnp.sqrt(acc) + EPSILON))

        for c in range(parts):
            for phase in (QUERY_OUT, QUERY_IN, GRAD_OUT, GRAD_IN):
                wait(q_send.at[s, c, others], send_sem.at[s, c, phase])
        wait(loss_all.at[s, others], send_sem.at[s, 0, LOSS])
        wait(negs.at[s, peers], nsend_sem.at[s, NEG])
        wait(negs.at[s, peers], nsend_sem.at[s, NEG_GRAD])
        return carry

    lax.fori_loop(0, steps, step, 0)

    for h in range(HALVES):
        wait(rel_recv.at[h, others], xrecv_sem.at[h, REL_SUM])
        mine = rel_recv[h, 0].astype(F32)
        for j in range(1, wide):
            mine = mine + rel_recv[h, j].astype(F32)
        rel_group_send[h] = mine
        narrow_start(
            lambda j: rel_group_send.at[h], lambda m: rel_group.at[h, m],
            xsend_sem.at[h, REL_GROUP], xrecv_sem.at[h, REL_GROUP],
        )
        rel_group[h, n] = mine
    for h in range(HALVES):
        wait(rel_group.at[h, peers], xrecv_sem.at[h, REL_GROUP])
        summed = rel_group[h, 0]
        for k in range(1, narrow):
            summed = summed + rel_group[h, k]
        rel_all_send[h] = summed.astype(BF16)
        wide_start(
            lambda j: rel_all_send.at[h], lambda m: rel_all.at[h, m],
            xsend_sem.at[h, REL_ALL], xrecv_sem.at[h, REL_ALL],
        )
        rel_all[h, w] = rel_all_send[h]
    for h in range(HALVES):
        wait(rel_all.at[h, others], xrecv_sem.at[h, REL_ALL])
        rel_out[:, h * half:(h + 1) * half] = rel_all[h].astype(F32).reshape(width, half)

    wait(tail_all.at[others], xsend_sem.at[0, TAIL_IDS])
    wait(neg_all.at[others], xsend_sem.at[0, NEG_IDS])
    for h in range(HALVES):
        wait(rel_recv.at[h, others], xsend_sem.at[h, REL_SUM])
        wait(rel_group.at[h, peers], xsend_sem.at[h, REL_GROUP])
        wait(rel_all.at[h, others], xsend_sem.at[h, REL_ALL])


def invert(order):
    positions = jnp.arange(order.shape[1], dtype=jnp.int32)
    return jnp.sum(
        jnp.where(order[:, :, None] == positions, positions[:, None], 0), axis=1, dtype=jnp.int32
    )


def on_device(
    wide, narrow,
    embeddings, accum, relation, head_index, tail_index, negative_index, partner, edge_count
):
    steps, edges = head_index.shape
    block, width = embeddings.shape
    negatives = negative_index.shape[1]
    depth = width // wide
    parts = max(1, min(2, edges // (16 * wide)))
    chunk = edges // parts
    piece = chunk // wide
    half = width // HALVES
    vmem = pl.BlockSpec(memory_space=pltpu.VMEM)
    smem = pl.BlockSpec(memory_space=pltpu.SMEM)
    pieces = pltpu.VMEM((steps, parts, wide, piece, width), BF16)
    landing = pltpu.VMEM((steps, wide, piece, width), BF16)
    group = pltpu.VMEM((steps, narrow, negatives, width), BF16)
    sems = pltpu.SemaphoreType.DMA
    new_emb, new_acc, rel_grad, losses = pl.pallas_call(
        functools.partial(kernel, wide, narrow, chunk),
        out_shape=(
            jax.ShapeDtypeStruct(embeddings.shape, F32),
            jax.ShapeDtypeStruct((1, block), F32),
            jax.ShapeDtypeStruct(relation.shape, F32),
            jax.ShapeDtypeStruct((steps, edges), F32),
        ),
        in_specs=[vmem] * 6 + [smem] * 3,
        out_specs=(vmem,) * 4,
        scratch_shapes=[
            pltpu.VMEM((wide, steps, edges), jnp.int32),
            pltpu.VMEM((wide, steps, negatives), jnp.int32),
            pltpu.VMEM((block, width), BF16),
            pltpu.VMEM((block, edges), BF16),
            pltpu.VMEM((block, edges), BF16),
            pltpu.VMEM((block, negatives), BF16),
            pltpu.VMEM((edges, width), BF16),
            pltpu.VMEM((edges, width), BF16),
            pieces, [landing] * parts, pieces, [landing] * parts,
            pieces, [landing] * parts, pieces, [landing] * parts,
            pltpu.VMEM((steps, 1, edges), F32),
            pltpu.VMEM((steps, wide, 1, edges), F32),
            group, group, group,
            pltpu.VMEM((edges, narrow * negatives), BF16),
            pltpu.VMEM((edges, width), BF16),
            pltpu.VMEM((block, width), F32),
            pltpu.VMEM(relation.shape, F32),
            pltpu.VMEM((HALVES, wide, depth, half), BF16),
            pltpu.VMEM((HALVES, wide, depth, half), BF16),
            pltpu.VMEM((HALVES, depth, half), F32),
            pltpu.VMEM((HALVES, narrow, depth, half), F32),
            pltpu.VMEM((HALVES, depth, half), BF16),
            pltpu.VMEM((HALVES, wide, depth, half), BF16),
            sems((steps, parts, 5)), sems((steps, parts, 5)), sems((steps, 2)), sems((steps, 2)),
            sems((HALVES, 5)), sems((HALVES, 5)),
        ],
        compiler_params=pltpu.CompilerParams(
            collective_id=0, has_side_effects=True, vmem_limit_bytes=56 * 1024 * 1024
        ),
    )(
        embeddings, accum.reshape(1, block), relation, head_index, tail_index, negative_index,
        partner, invert(partner), edge_count,
    )
    return new_emb, new_acc.reshape(block), rel_grad, losses


def solution(mesh):
    both = ("wide", "narrow")
    in_specs = (
        P(both, None), P(both), P(), P(None, both), P(None, both), P(None, both), P(), P(None, both)
    )
    out_specs = (P(both, None), P(both), P(), P(None, both))
    return jax.shard_map(
        functools.partial(on_device, mesh.shape["wide"], mesh.shape["narrow"]),
        mesh=mesh, in_specs=in_specs, out_specs=out_specs, check_vma=False,
    )
```

time: 150 us -> 141 us (0.940)
  Pallas kernels: 141 us -> 132 us
    pallas_call x1, Pallas kernels: 141 us -> 132 us  [on_device(): pl.pallas_call(functools.partial(kernel, wide, narrow, chunk), out_shape=...]
where the time goes in v2:
time: 141 us; the launch traced here: 140 us
  Pallas kernels  132 us (94%)
  local copies, waits for them, and re-layouts  5.83 us (4%)
    pallas_call x1, Pallas kernels, on_device(): pl.pallas_call(functools.partial(kernel, wide, narrow, chunk), out_shape=...  132 us
    unnamed x15, local copies, waits for them, and re-layouts  5.83 us

profile of v2, /device:TPU:0, one launch (start us, length us, event | category | flops | bytes accessed | tf_op | source)
XLA Modules:
  0.0 139.6 jit_solution(12255494681318685068)
XLA Ops:
  0.6 0.0 copy-start.4
  0.6 0.6 copy-done.4
  1.3 0.0 copy-start.2
  1.3 0.6 copy.13.count_ref
  1.9 0.0 copy-done.2
  2.0 0.6 select_reduce_fusion.inverse_ref
  2.6 132.4 %shard_map.111 = (f32[512,512]{1,0:T(8,128)}, f32[1,512]{1,0:T(1,128)}, f32[512,512]{1,0:T(8,128)}, f32[2,512]{1,0:T(2,128)}) custom-call(f32[512,512]{1,0:T(8,128)} %emb_ref.1, f32[1,512]{1,0:T(1,128)} %bitcast.2, bf16[512,512]{1,0:T(8,128)(2,1)} %rel_ref.1, s32[2,512]{1,0:T(2,128)} %head_ref.1, s32[2,512]{1,0:T(2,128)} %tail_ref.1, s32[2,256]{1,0:T(2,128)} %neg_ref.1, ...), custom_call_target="tpu_custom_call" | custom-call | tf_op jit(solution)/shard_map/pallas_call | solution.py:311
  135.1 0.0 copy-start.3
  135.1 0.0 copy-start
  135.1 2.4 %copy.18 = f32[512,512]{1,0:T(8,128)} copy(f32[512,512]{1,0:T(8,128)} %get-tuple-element.16) | data formatting | bytes 2097152
  137.4 0.0 copy-done.3
  137.4 0.6 copy.19
  138.0 0.0 copy-done
  138.0 0.0 copy-start.1
  138.0 1.0 copy.20
  139.0 0.0 copy-done.1
  139.0 0.6 copy.21
Async XLA Ops:
  0.6 0.7 copy-start.4
  1.3 0.7 copy-start.2
  135.1 2.4 %copy-start.3 = (f32[1,512]{1,0:T(1,128)S(1)}, f32[1,512]{1,0:T(1,128)}, u32[]{:S(2)}) copy-start(f32[1,512]{1,0:T(1,128)} %get-tuple-element.9) | copy-start | bytes 6148
  135.1 2.9 %copy-start = (f32[512,512]{1,0:T(8,128)S(1)}, f32[512,512]{1,0:T(8,128)}, u32[]{:S(2)}) copy-start(f32[512,512]{1,0:T(8,128)} %get-tuple-element.18) | copy-start | bytes 3145732
  138.0 1.0 copy-start.1

commit v3 on v2

--- a/solution.py
+++ b/solution.py
@@ -74,7 +74,8 @@
 
     def wide_start(source, target, ssem, rsem):
         def go(i, carry):
-            j = lax.rem(w + i, wide)
+            far = 1 + lax.rem(i - 1 + (wide - 1) // 2, wide - 1)
+            j = lax.rem(w + far, wide)
             pltpu.make_async_remote_copy(
                 src_ref=source(j), dst_ref=target(w), send_sem=ssem, recv_sem=rsem,
                 device_id=(j, n), device_id_type=MESH,

time: 141 us -> 143 us (1.014)
  Pallas kernels: 132 us -> 136 us
    pallas_call x1, Pallas kernels: 132 us -> 136 us  [on_device(): pl.pallas_call(functools.partial(kernel, wide, narrow, chunk), out_shape=...]
where the time goes in v3:
time: 143 us
  Pallas kernels  136 us (95%)
  local copies, waits for them, and re-layouts  5.83 us (4%)
    pallas_call x1, Pallas kernels, on_device(): pl.pallas_call(functools.partial(kernel, wide, narrow, chunk), out_shape=...  136 us
    unnamed x15, local copies, waits for them, and re-layouts  5.83 us

profile of v3, /device:TPU:0, one launch (start us, length us, event | category | flops | bytes accessed | tf_op | source)
XLA Modules:
  0.0 143.0 jit_solution(14926294834529926070)
XLA Ops:
  0.6 0.0 copy-start.4
  0.6 0.6 copy-done.4
  1.3 0.0 copy-start.2
  1.3 0.6 copy.13.count_ref
  1.9 0.0 copy-done.2
  2.0 0.6 select_reduce_fusion.inverse_ref
  2.6 135.9 %shard_map.111 = (f32[512,512]{1,0:T(8,128)}, f32[1,512]{1,0:T(1,128)}, f32[512,512]{1,0:T(8,128)}, f32[2,512]{1,0:T(2,128)}) custom-call(f32[512,512]{1,0:T(8,128)} %emb_ref.1, f32[1,512]{1,0:T(1,128)} %bitcast.2, bf16[512,512]{1,0:T(8,128)(2,1)} %rel_ref.1, s32[2,512]{1,0:T(2,128)} %head_ref.1, s32[2,512]{1,0:T(2,128)} %tail_ref.1, s32[2,256]{1,0:T(2,128)} %neg_ref.1, ...), custom_call_target="tpu_custom_call" | custom-call | tf_op jit(solution)/shard_map/pallas_call | solution.py:312
  138.5 0.0 copy-start.3
  138.5 0.0 copy-start
  138.5 2.4 %copy.18 = f32[512,512]{1,0:T(8,128)} copy(f32[512,512]{1,0:T(8,128)} %get-tuple-element.16) | data formatting | bytes 2097152
  140.9 0.0 copy-done.3
  140.9 0.6 copy.19
  141.4 0.0 copy-done
  141.4 0.0 copy-start.1
  141.4 1.0 copy.20
  142.4 0.0 copy-done.1
  142.4 0.6 copy.21
Async XLA Ops:
  0.6 0.7 copy-start.4
  1.3 0.7 copy-start.2
  138.5 2.4 %copy-start.3 = (f32[1,512]{1,0:T(1,128)S(1)}, f32[1,512]{1,0:T(1,128)}, u32[]{:S(2)}) copy-start(f32[1,512]{1,0:T(1,128)} %get-tuple-element.9) | copy-start | bytes 6148
  138.5 2.9 %copy-start = (f32[512,512]{1,0:T(8,128)S(1)}, f32[512,512]{1,0:T(8,128)}, u32[]{:S(2)}) copy-start(f32[512,512]{1,0:T(8,128)} %get-tuple-element.18) | copy-start | bytes 3145732
  141.4 1.0 copy-start.1
